TPU v7x, 32 devices: a whole 2x2x4 slice. The times are simulated.
32 devices in a mesh: dp: 8 (over y, x, core), seq: 4 (over z).
Axes of the slice: x: 2, y: 2, z: 4, core: 2. Of those that a mesh axis runs over, the one named last changes fastest.
Arguments:
- queries: bfloat16 [8192, 8192], P(('dp', 'seq')), may hold values from -60 to 60
- keys: bfloat16 [8192, 1024], P(('dp', 'seq')), may hold values from -60 to 60
- values: bfloat16 [8192, 1024], P(('dp', 'seq')), may hold values from -6 to 6
- plan: int32 [8192], P(('dp', 'seq')), may hold values from 0 to 8191, as said below
- segment_ids: int32 [8192], P(('dp', 'seq')), may hold values from 0 to 63, as said below
Outputs:
- attended: bfloat16 [8192, 8192], P(('dp', 'seq'))
Inputs may be any that keep to these rules, and one draw needn't show every extreme that they name: `plan`: A permutation of the owner rows. The rows of one device go exactly 8 to each device (owner rows d * 256 to (d + 1) * 256 - 1 belong to device d), in random order among the device's rows. `segment_ids`: documents are runs of equal ids that never fall; every length is a multiple of 128; no document crosses a boundary of the aligned blocks of 1024 owner rows; one document fills a whole block.
All inputs are finite; a program needn't handle non-finite values.
Results may differ from a plain program's by a relative error of at most 0.0053.
Values may be sent and summed in bfloat16 or wider, within the bound.
A program may use at most 128 MiB of HBM per device.

v0:
```python
import jax
import jax.numpy as jnp
from jax import lax
from jax.sharding import PartitionSpec as P

H = 64
KVH = 8
HD = 128


theta_base = 500000.0
tile_rows = 512


def doc_positions(segment_ids):
    places = jnp.arange(segment_ids.shape[0], dtype=jnp.int32)
    starts = jnp.concatenate([jnp.ones((1,), jnp.bool_), segment_ids[1:] != segment_ids[:-1]])
    first = lax.cummax(jnp.where(starts, places, jnp.zeros_like(places)), axis=0)
    return (places - first, first)


def rotate(source, positions):
    width = source.shape[-1]
    half = width // 2
    freqs = theta_base ** (-2.0 * jnp.arange(half, dtype=jnp.float32) / width)
    angles = positions.astype(jnp.float32)[:, None] * freqs[None, :]
    cosine = jnp.cos(angles)[:, None, :]
    sine = jnp.sin(angles)[:, None, :]
    floats = source.astype(jnp.float32)
    lower = floats[..., :half]
    upper = floats[..., half:]
    turned = jnp.concatenate(
        [lower * cosine - upper * sine, upper * cosine + lower * sine], axis=-1
    )
    return turned.astype(jnp.bfloat16)


def tiles_over(block, block_ids, query_rows, group_k, group_v, group_ids, lowest, upper):
    kv_count = block.shape[1]
    per_kv = block.shape[2]
    width = block.shape[3]
    count = block.shape[0]
    scale = width ** (-0.5)

    def one_tile(tile, carry):
        peak, totals, mixed = carry
        anchor = tile * tile_rows
        tile_k = lax.dynamic_slice_in_dim(group_k, anchor, tile_rows, 0)
        tile_v = lax.dynamic_slice_in_dim(group_v, anchor, tile_rows, 0)
        tile_ids = lax.dynamic_slice_in_dim(group_ids, anchor, tile_rows, 0)
        key_rows = anchor + jnp.arange(tile_rows, dtype=jnp.int32)
        scores = (
            jnp.einsum("qkgd,tkd->kgqt", block, tile_k, preferred_element_type=jnp.float32) * scale
        )
        allowed = (key_rows[None, :] <= query_rows[:, None]) & (
            tile_ids[None, :] == block_ids[:, None]
        )
        scores = jnp.where(allowed, scores, -jnp.inf)
        raised = jnp.maximum(peak, jnp.max(scores, axis=-1))
        weights = jnp.exp(scores - raised[..., None])
        shrink = jnp.exp(peak - raised)
        totals = totals * shrink + jnp.sum(weights, axis=-1)
        added = jnp.einsum(
            "kgqt,tkd->kgqd",
            weights.astype(jnp.bfloat16),
            tile_v,
            preferred_element_type=jnp.float32,
        )
        mixed = mixed * shrink[..., None] + added
        return (raised, totals, mixed)

    initial = (
        jnp.full((kv_count, per_kv, count), -1e30, jnp.float32),
        jnp.zeros((kv_count, per_kv, count), jnp.float32),
        jnp.zeros((kv_count, per_kv, count, width), jnp.float32),
    )
    peak, totals, mixed = lax.fori_loop(lowest, upper, one_tile, initial)
    result = mixed / totals[..., None]
    return jnp.transpose(result, (2, 0, 1, 3)).astype(jnp.bfloat16)


def settle(arrived, rows_here):
    where_rows = arrived[3].reshape(rows_here)
    placement = jnp.argsort(where_rows)
    own_q = arrived[0].reshape(rows_here, -1)[placement]
    own_k = arrived[1].reshape(rows_here, -1)[placement]
    own_v = arrived[2].reshape(rows_here, -1)[placement]
    return (where_rows, own_q, own_k, own_v)


def per_device(queries, keys, values, plan, segment_ids):
    rows_here = queries.shape[0]
    seq_count = lax.axis_size("seq")
    dp_count = lax.axis_size("dp")
    devices = seq_count * dp_count
    share = rows_here // devices
    per_kv = H // KVH
    group_ids = lax.all_gather(segment_ids, "seq", axis=0, tiled=True)
    positions, first = doc_positions(group_ids)
    targets = plan // rows_here
    order = jnp.argsort(targets, stable=True)
    sorted_q = queries[order]
    sorted_k = keys[order]
    sorted_v = values[order]
    owner_local = (plan % rows_here)[order].reshape(devices, share)
    arrived = (
        lax.all_to_all(
            sorted_q.reshape(devices, share, -1),
            ("dp", "seq"),
            split_axis=0,
            concat_axis=0,
            tiled=True,
        ),
        lax.all_to_all(
            sorted_k.reshape(devices, share, -1),
            ("dp", "seq"),
            split_axis=0,
            concat_axis=0,
            tiled=True,
        ),
        lax.all_to_all(
            sorted_v.reshape(devices, share, -1),
            ("dp", "seq"),
            split_axis=0,
            concat_axis=0,
            tiled=True,
        ),
        lax.all_to_all(owner_local, ("dp", "seq"), split_axis=0, concat_axis=0, tiled=True),
    )
    where_rows, own_q, own_k, own_v = settle(arrived, rows_here)
    here = lax.axis_index("seq") * rows_here
    local_pos = lax.dynamic_slice_in_dim(positions, here, rows_here, 0)
    local_ids = lax.dynamic_slice_in_dim(group_ids, here, rows_here, 0)
    rot_q = rotate(own_q.reshape(rows_here, H, HD), local_pos).reshape(rows_here, KVH, per_kv, HD)
    rot_k = rotate(own_k.reshape(rows_here, KVH, HD), local_pos)
    group_k, group_v = (
        lax.all_gather(rot_k, "seq", axis=0, tiled=True),
        lax.all_gather(own_v.reshape(rows_here, KVH, HD), "seq", axis=0, tiled=True),
    )
    query_rows = here + jnp.arange(rows_here, dtype=jnp.int32)
    upper = (here + rows_here - 1) // tile_rows + 1
    lowest = jnp.zeros((), jnp.int32)
    owner_out = tiles_over(
        rot_q, local_ids, query_rows, group_k, group_v, group_ids, lowest, upper
    ).reshape(rows_here, -1)
    leaving = owner_out[where_rows].reshape(devices, share, -1)
    home = lax.all_to_all(leaving, ("dp", "seq"), split_axis=0, concat_axis=0, tiled=True).reshape(
        rows_here, -1
    )
    return jnp.zeros_like(home).at[order].set(home)


def solution(mesh):
    return jax.shard_map(
        per_device,
        mesh=mesh,
        in_specs=(
            P(("dp", "seq"), None),
            P(("dp", "seq"), None),
            P(("dp", "seq"), None),
            P(("dp", "seq")),
            P(("dp", "seq")),
        ),
        out_specs=P(("dp", "seq"), None),
        check_vma=False,
    )
```

profile of v0, /device:TPU:1, one launch (start us, length us, event | category | flops | bytes accessed | tf_op | source)
XLA Modules:
  0.0 494.8 jit_solution(781167705408558086)
XLA Ops:
  6.5 0.8 and_select_fusion
  7.3 3.2 sort.34
  10.5 1.9 gather_fusion.1
  12.5 0.7 all_to_all.19
  13.1 7.1 %all-to-all-start.1 = ((s32[32,1,8]{2,1,0:T(1,128)}), s32[32,1,8]{2,1,0:T(1,128)S(1)}, u32[]{:S(2)}, u32[]{:S(2)}) async-start(s32[32,1,8]{2,1,0:T(1,128)} %bitcast.4), calls=%async_computation.1 | async-start | bytes 32768 | tf_op jit(solution)/shard_map/all_to_all | solution.py:128
  20.2 2.0 gather_fusion.5
  22.2 4.7 all-to-all-done.1
  26.9 3.0 all-to-all-start.3
  29.9 2.0 gather_fusion
  31.9 13.4 %all-to-all-done.3 = bf16[32,8,1024]{2,1,0:T(8,128)(2,1)S(1)} async-done(((bf16[32,8,1024]{2,1,0:T(8,128)(2,1)}), bf16[32,8,1024]{2,1,0:T(8,128)(2,1)S(1)}, u32[]{:S(2)}, u32[]{:S(2)}) %all-to-all-start.3) | async-done | bytes 524320 | tf_op jit(solution)/shard_map/all_to_all | solution.py:121
  45.3 3.1 all-to-all-start
  48.4 11.7 %gather_fusion.3 = bf16[256,8192]{1,0:T(8,128)(2,1)} fusion(bf16[256,8192]{1,0:T(8,128)(2,1)} %param.7, s32[1024]{0:T(1024)S(1)} %pad_clamp_fusion.2), kind=kCustom, calls=%fused_computation.3 | custom fusion | bytes 8389632 | tf_op jit(solution)/shard_map/gather | solution.py:102
  60.2 3.5 all-to-all-done
  63.7 3.3 all-to-all-start.2
  67.0 0.0 all-gather.6.cloned.1.call-start
  67.1 0.5 broadcast.161
  67.6 0.7 reduce.7
  68.3 0.1 reshape.157
  68.4 3.2 sort.35
  71.5 1.2 gather_fusion.6
  72.7 0.9 copy_bitcast_fusion.1
  73.6 0.0 all-gather.6.cloned.1.call-update
  73.6 0.0 all-gather.4.cloned.1.call-start
  73.7 100.3 %all-gather = s32[4,1,256]{2,1,0:T(1,128)S(1)} all-gather(s32[1,1,256]{2,1,0:T(1,128)S(1)} %bitcast.93), channel_id=1, replica_groups=mesh['dp'=8,'seq'=4] {'seq'}, dimensions={0}, use_global_device_ids=true | all-gather | bytes 5120 | tf_op jit(solution)/shard_map/all_gather | solution.py:98
  174.0 0.1 slice_compare_fusion
  174.1 0.1 add_select_fusion
  174.2 0.3 reduce-window.9
  174.5 0.1 slice.28
  174.6 0.1 slice_reduce_fusion
  174.7 0.1 bitcast_subtract_fusion
  174.8 0.1 dynamic-slice_convert_fusion
  174.9 0.5 multiply_cosine_fusion
  175.4 1.2 gather_fusion.2
  176.6 0.1 convert_bitcast_fusion.1
  176.7 0.2 copy.34
  176.9 0.3 fusion.23
  177.2 0.4 subtract_convert_fusion.1
  177.7 1.1 pad_maximum_fusion.1
  178.8 0.1 dynamic_slice.15
  178.9 0.1 reshape.165
  179.0 0.6 pad_clamp_fusion
  179.6 13.0 %all-to-all-done.2 = bf16[32,8,8192]{2,1,0:T(8,128)(2,1)} async-done(((bf16[32,8,8192]{2,1,0:T(8,128)(2,1)}), bf16[32,8,8192]{2,1,0:T(8,128)(2,1)}, u32[]{:S(2)}, u32[]{:S(2)}) %all-to-all-start.2) | async-done | bytes 4194336 | tf_op jit(solution)/shard_map/all_to_all | solution.py:107
  192.6 11.7 %gather_fusion.4 = bf16[256,8192]{1,0:T(8,128)(2,1)} fusion(bf16[256,8192]{1,0:T(8,128)(2,1)} %bitcast.8, s32[1024]{0:T(1024)S(1)} %pad_clamp_fusion.1), kind=kCustom, calls=%fused_computation.4 | custom fusion | bytes 8389632 | tf_op jit(solution)/shard_map/gather | solution.py:85
  204.3 3.2 convert_bitcast_fusion
  207.5 1.8 copy.35
  209.3 3.4 subtract_convert_fusion
  212.7 2.7 copy.24
  215.4 2.7 copy.25
  218.1 3.7 pad_maximum_fusion
  221.8 23.6 %all-gather.4.cloned.1.call-done = bf16[1024,8,128]{2,0,1:T(8,128)(2,1)} async-done(((bf16[256,8,128]{2,0,1:T(8,128)(2,1)}), bf16[1024,8,128]{2,0,1:T(8,128)(2,1)}) %all-gather.4.cloned.1.call-update) | async-done | bytes 2097168 | tf_op jit(solution)/shard_map/all_gather | solution.py:137
  245.4 4.2 broadcast_in_dim.24
  249.6 49.7 %while.15 = (s32[]{:T(128)}, f32[8,8,256]{2,1,0:T(8,128)S(1)}, f32[8,8,256]{2,1,0:T(8,128)S(1)}, f32[8,8,256,128]{3,2,1,0:T(8,128)}, s32[]{:T(128)}, /*index=5*/...) while((s32[]{:T(128)}, f32[8,8,256]{2,1,0:T(8,128)S(1)}, ...), condition=%wide.region_7.8_spmd.clone, body=%wide.region_4.7_spmd.clone.sunk | while | flops 4391863296 | bytes 200815920 | solution.py:77
  249.7 0.1 dynamic_slice.36
  249.7 0.2 compare_and_fusion.2
  249.9 15.3 %fusion.34 = (f32[8,8,256]{2,1,0:T(8,128)S(1)}, f32[8,512,256,8]{2,1,3,0:T(8,128)}) fusion(pred[256,512]{0,1:T(8,128)(4,1)S(1)} %compare_and_fusion.2, bf16[256,8,8,128]{3,0,2,1:T(8,128)(2,1)} %get-tuple-element.246, bf16[1024,8,128]{2,0,1:T(8,128)(2,1)S(1)} %get-tuple-element.245, s32[]{:T(128)S(6)} %select_n.89), kind=kOutput, calls=%fused_computation.14.clone.1 | convolution fusion | flops 2172633088 | bytes 38993924 | tf_op jit(solution)/shard_map/while/body/qkgd,tkd->kgqt/dot_general | solution.py:53
  265.3 15.7 %fusion.35 = f32[8,8,256]{2,1,0:T(8,128)S(1)} fusion(f32[8,512,256,8]{2,1,3,0:T(8,128)} %get-tuple-element.205, f32[8,8,256]{2,1,0:T(8,128)S(1)} %max.5, pred[256,512]{0,1:T(8,128)(4,1)S(1)} %compare_and_fusion.2), kind=kLoop, calls=%fused_computation.13.clone.1 | loop fusion | flops 33538048 | bytes 33816576 | tf_op jit(solution)/shard_map/while/body/reduce_sum | solution.py:62
  281.1 15.1 %multiply_add_fusion.5 = f32[8,8,256,128]{3,2,1,0:T(8,128)S(1)} fusion(f32[8,8,256,128]{3,2,1,0:T(8,128)S(1)} %copy-done.3, f32[8,8,256]{2,1,0:T(8,128)S(1)} %get-tuple-element.207, f32[8,512,256,8]{2,1,3,0:T(8,128)} %get-tuple-element.205, f32[8,8,256]{2,1,0:T(8,128)S(1)} %max.5, pred[256,512]{0,1:T(8,128)(4,1)S(1)} %compare_and_fusion.2, ...), kind=kOutput, calls=%fused_computation.17.clone.1 | convolution fusion | flops 2185232384 | bytes 51642372 | tf_op jit(solution)/shard_map/while/body/kgqt,tkd->kgqd/dot_general | solution.py:63
  296.2 3.2 copy-done.4
  299.4 5.4 %fusion.21 = bf16[256,8,8,128]{3,0,2,1:T(8,128)(2,1)S(1)} fusion(f32[8,8,256,128]{3,2,1,0:T(8,128)} %get-tuple-element.68, f32[8,8,256]{2,1,0:T(8,128)S(1)} %get-tuple-element.69), kind=kLoop, calls=%fused_computation.40 | loop fusion | flops 4194304 | bytes 12648448 | tf_op jit(solution)/shard_map/convert_element_type | solution.py:79
  304.8 2.7 copy.27
  307.5 10.2 %copy.43 = bf16[32,8,64,128]{3,1,2,0:T(8,128)(2,1)} copy(bf16[32,8,64,128]{3,2,1,0:T(8,128)(2,1)S(1)} %bitcast.84) | data formatting | bytes 8388608
  317.7 12.2 %gather_fusion.7 = bf16[256,8192]{1,0:T(8,128)(2,1)} fusion(bf16[256,8192]{1,0:T(8,128)(2,1)} %bitcast.78, s32[1024]{0:T(1024)} %pad_clamp_fusion), kind=kCustom, calls=%fused_computation.7 | custom fusion | bytes 8389632 | tf_op jit(solution)/shard_map/gather | solution.py:146
  329.9 147.7 %all_to_all.29 = bf16[32,8,8192]{2,1,0:T(8,128)(2,1)} all-to-all(bf16[32,8,8192]{2,1,0:T(8,128)(2,1)} %bitcast.86), channel_id=1, replica_groups=mesh['dp'=8,'seq'=4] {'dp','seq'}, dimensions={0} | all-to-all | bytes 8388608 | tf_op jit(solution)/shard_map/all_to_all | solution.py:147
  477.6 10.1 %scatter_custom_fusion = bf16[256,8192]{1,0:T(8,128)(2,1)} fusion(s32[256]{0:T(256)} %copy-done.6, bf16[32,8,8192]{2,1,0:T(8,128)(2,1)} %all_to_all.29, bf16[]{:T(256)} %constant.71.clone.1), kind=kCustom, calls=%fused_computation.38 | custom fusion | bytes 8389120 | tf_op jit(solution)/shard_map/scatter | solution.py:150
  (35 shorter events, 0.2 us)
Async XLA Ops:
  6.5 13.7 %copy-start = (bf16[256,1024]{1,0:T(8,128)(2,1)S(1)}, bf16[256,1024]{1,0:T(8,128)(2,1)}, u32[]{:S(2)}) copy-start(bf16[256,1024]{1,0:T(8,128)(2,1)} %param.9) | copy-start | bytes 1572868
  6.5 23.4 %copy-start.2 = (bf16[256,1024]{1,0:T(8,128)(2,1)S(1)}, bf16[256,1024]{1,0:T(8,128)(2,1)}, u32[]{:S(2)}) copy-start(bf16[256,1024]{1,0:T(8,128)(2,1)} %param.8) | copy-start | bytes 1572868
  10.5 2.6 copy-start.6
  13.1 13.8 %all-to-all-start.1 = ((s32[32,1,8]{2,1,0:T(1,128)}), s32[32,1,8]{2,1,0:T(1,128)S(1)}, u32[]{:S(2)}, u32[]{:S(2)}) async-start(s32[32,1,8]{2,1,0:T(1,128)} %bitcast.4), calls=%async_computation.1 | async-start | bytes 32768 | tf_op jit(solution)/shard_map/all_to_all | solution.py:128
  26.9 18.4 %all-to-all-start.3 = ((bf16[32,8,1024]{2,1,0:T(8,128)(2,1)}), bf16[32,8,1024]{2,1,0:T(8,128)(2,1)S(1)}, u32[]{:S(2)}, u32[]{:S(2)}) async-start(bf16[32,8,1024]{2,1,0:T(8,128)(2,1)} %bitcast.11), calls=%async_computation.3 | async-start | bytes 1048576 | tf_op jit(solution)/shard_map/all_to_all | solution.py:121
  45.3 18.4 %all-to-all-start = ((bf16[32,8,1024]{2,1,0:T(8,128)(2,1)}), bf16[32,8,1024]{2,1,0:T(8,128)(2,1)S(1)}, u32[]{:S(2)}, u32[]{:S(2)}) async-start(bf16[32,8,1024]{2,1,0:T(8,128)(2,1)} %bitcast.2), calls=%async_computation | async-start | bytes 1048576 | tf_op jit(solution)/shard_map/all_to_all | solution.py:114
  60.2 13.5 %copy-start.7 = (s32[256]{0:T(256)S(1)}, s32[256]{0:T(256)}, u32[]{:S(2)}) copy-start(s32[256]{0:T(256)} %param.11) | copy-start | bytes 3076
  63.7 128.9 %all-to-all-start.2 = ((bf16[32,8,8192]{2,1,0:T(8,128)(2,1)}), bf16[32,8,8192]{2,1,0:T(8,128)(2,1)}, u32[]{:S(2)}, u32[]{:S(2)}) async-start(bf16[32,8,8192]{2,1,0:T(8,128)(2,1)} %bitcast.85), calls=%async_computation.2 | async-start | bytes 8388608 | tf_op jit(solution)/shard_map/all_to_all | solution.py:107
  67.0 154.8 %all-gather.6.cloned.1.call-start = ((), (), s32[]{:S(2)}) async-start(), calls=%async_computation.6 | async-start | bytes 2621440 | tf_op jit(solution)/shard_map/all_gather | solution.py:138
  73.6 171.8 %all-gather.4.cloned.1.call-start = ((), (), s32[]{:S(2)}) async-start(), calls=%async_computation.5 | async-start | bytes 2621440 | tf_op jit(solution)/shard_map/all_gather | solution.py:137
  245.4 4.2 copy-start.5
  265.3 15.8 %copy-start.3 = (f32[8,8,256,128]{3,2,1,0:T(8,128)S(1)}, f32[8,8,256,128]{3,2,1,0:T(8,128)}, u32[]{:S(2)}) copy-start(f32[8,8,256,128]{3,2,1,0:T(8,128)} %get-tuple-element.226) | copy-start | bytes 25165828 | tf_op jit(solution)/shard_map/while
  265.3 15.8 %copy-start.8 = (bf16[1024,8,128]{2,0,1:T(8,128)(2,1)S(1)}, bf16[1024,8,128]{2,0,1:T(8,128)(2,1)}, u32[]{:S(2)}) copy-start(bf16[1024,8,128]{2,0,1:T(8,128)(2,1)} %get-tuple-element.247) | copy-start | bytes 6291460 | tf_op jit(solution)/shard_map/while
  296.2 3.2 copy-start.4
  329.9 157.9 %copy-start.1 = (bf16[256,1024]{1,0:T(8,128)(2,1)S(1)}, bf16[256,1024]{1,0:T(8,128)(2,1)}, u32[]{:S(2)}) copy-start(bf16[256,1024]{1,0:T(8,128)(2,1)} %param.9) | copy-start | bytes 1572868
Sparse Core Ops, SparseCore 0:
  73.8 99.2 all-gather.5
  178.9 66.4 all-gather.3
where the time goes:
time: 504 us; the launch traced here: 495 us
  blocking collectives  248 us (49%)
  local copies, waits for them, and re-layouts  84.7 us (17%)
  waiting for transfers between devices  58.3 us (12%)
  other arithmetic  42.9 us (9%)
  matrix products  30.4 us (6%)
  starting transfers between devices  16.6 us (3%)
  between operations  13.8 us (3%)
    all_to_all x1, blocking collectives, per_device(): lax.all_to_all(leaving, ('dp', 'seq'), split_axis=0, concat_axis=0, tiled...  148 us
    all_gather x1, blocking collectives, per_device(): group_ids = lax.all_gather(segment_ids, 'seq', axis=0, tiled=True)  100 us
    all_gather x1, waiting for transfers between devices, per_device(): lax.all_gather(rot_k, 'seq', axis=0, tiled=True)  23.6 us
    reduce_sum x1, other arithmetic, one_tile(): totals = totals * shrink + jnp.sum(weights, axis=-1)  15.7 us
    dot_general x1, matrix products, one_tile(): jnp.einsum('qkgd,tkd->kgqt', block, tile_k, preferred_element_type=jnp.fl...  15.3 us
    dot_general x1, matrix products, one_tile(): jnp.einsum('kgqt,tkd->kgqd', weights.astype(jnp.bfloat16), tile_v, prefer...  15.1 us
    all_to_all x1, waiting for transfers between devices, per_device(): lax.all_to_all(sorted_v.reshape(devices, share, -1), ('dp', 'seq'), split...  13.4 us
    all_to_all x1, waiting for transfers between devices, per_device(): lax.all_to_all(sorted_q.reshape(devices, share, -1), ('dp', 'seq'), split...  13 us
  transfers between devices with their start and end apart: 6, of which 5 were waited for; matrix products, arithmetic and copies ran while one was open for 11% of the time, Pallas kernels for 0%

commit v1 on v0

v1 whole, which is shorter than its diff:
```python
import functools

import jax
import jax.numpy as jnp
from jax import lax
from jax.experimental import pallas as pl
from jax.experimental.pallas import tpu as pltpu
from jax.sharding import PartitionSpec as P

H = 64
KVH = 8
HD = 128
theta_base = 500000.0
UNIT = 128
META = 128
LOG2E = 1.4426950408889634


def onehot_rows(index, count):
    return (index[None, :] == jnp.arange(count, dtype=jnp.int32)[:, None]).astype(jnp.bfloat16)


def permuted(onehot, rows):
    return jnp.dot(onehot, rows, preferred_element_type=jnp.float32).astype(jnp.bfloat16)


def turns(positions):
    half = HD // 2
    freqs = theta_base ** (-2.0 * jnp.arange(half, dtype=jnp.float32) / HD)
    angles = positions.astype(jnp.float32)[:, None] * freqs[None, :]
    cosine, sine = jnp.cos(angles), jnp.sin(angles)
    return (
        jnp.concatenate([cosine, cosine], axis=-1),
        jnp.concatenate([-sine, sine], axis=-1),
    )


def attend(seqs, dps, q_ref, k_ref, v_ref, cq, sq, ck, sk, bias, o_ref, ks, vs, ob):
    rows = q_ref.shape[0]
    chunk = rows // seqs
    share = chunk // dps
    per_kv = q_ref.shape[1] // HD

    def arrival(s):
        inner = s % chunk
        return (inner // share) * (seqs * share) + (s // chunk) * share + inner % share

    row = lax.broadcasted_iota(jnp.int32, (rows, rows), 0)
    col = lax.broadcasted_iota(jnp.int32, (rows, rows), 1)
    sort = jnp.where(col == arrival(row), 1.0, 0.0).astype(jnp.bfloat16)
    unsort = jnp.where(row == arrival(col), 1.0, 0.0).astype(jnp.bfloat16)

    def dot(a, b):
        return jnp.dot(a, b, preferred_element_type=jnp.float32)

    def turn(x, c, s):
        return (x * c + pltpu.roll(x, HD // 2, 1) * s).astype(jnp.bfloat16)

    for p in range(seqs):
        part = turn(dot(sort, k_ref[p]), ck[p], sk[p])
        part_v = dot(sort, v_ref[p]).astype(jnp.bfloat16)
        for z in range(seqs):
            ks[z * rows + p * chunk : z * rows + (p + 1) * chunk] = part[z * chunk : (z + 1) * chunk]
            vs[z * rows + p * chunk : z * rows + (p + 1) * chunk] = part_v[z * chunk : (z + 1) * chunk]
    turned = []
    for g in range(per_kv):
        x = dot(sort, q_ref[:, g * HD : (g + 1) * HD])
        turned.append(turn(x, cq[...], sq[...]))
    for c in range(seqs):
        reach = (c + 1) * rows
        block = jnp.concatenate([t[c * chunk : (c + 1) * chunk] for t in turned], axis=0)
        s = lax.dot_general(
            block, ks[:reach], (((1,), (1,)), ((), ())), preferred_element_type=jnp.float32
        )
        s = s.reshape(per_kv, chunk, reach) * (HD ** -0.5 * LOG2E)
        s = s + bias[c * chunk : (c + 1) * chunk, :reach][None]
        e = jnp.exp2(s - jnp.max(s, axis=-1, keepdims=True))
        total = jnp.sum(e, axis=-1, keepdims=True).reshape(per_kv * chunk, 1)
        mixed = dot(e.astype(jnp.bfloat16).reshape(per_kv * chunk, reach), vs[:reach]) / total
        mixed = mixed.astype(jnp.bfloat16)
        for g in range(per_kv):
            ob[c * chunk : (c + 1) * chunk, g * HD : (g + 1) * HD] = mixed[g * chunk : (g + 1) * chunk]
    o_ref[...] = dot(unsort, ob[...]).astype(jnp.bfloat16)


def per_device(queries, keys, values, plan, segment_ids):
    rows = queries.shape[0]
    seqs = lax.axis_size("seq")
    dps = lax.axis_size("dp")
    group = rows * seqs
    share = rows // (seqs * dps)
    chunk = rows // seqs
    per_kv = H // KVH
    unit_ids = lax.all_gather(segment_ids[::UNIT], "seq", axis=0, tiled=True)
    units = unit_ids.shape[0]
    target = plan // rows
    places = jnp.arange(rows, dtype=jnp.int32)
    same = (target[:, None] == target[None, :]) & (places[None, :] < places[:, None])
    slot = target * share + jnp.sum(same.astype(jnp.int32), axis=1)
    onehot = onehot_rows(slot, rows)
    spot = plan % group
    lane = jnp.arange(META, dtype=jnp.int32)[None, :]
    meta = jnp.where(lane == 0, (spot // 32)[:, None], jnp.where(lane == 1, (spot % 32)[:, None], 0))
    kv = jnp.concatenate([keys, values, meta.astype(jnp.bfloat16)], axis=1)

    def swap(x):
        wide = x.shape[-1]
        return lax.all_to_all(
            x.reshape(dps, rows // dps, wide), "dp", split_axis=0, concat_axis=0, tiled=True
        ).reshape(rows, wide)

    kv_here = swap(permuted(onehot, kv))
    q_here = swap(permuted(onehot, queries))
    kv_all = lax.all_gather(kv_here, "seq", axis=0)
    marks = kv_all[:, :, 2 * KVH * HD : 2 * KVH * HD + 2].astype(jnp.int32)
    key_spot = (marks[..., 0] * 32 + marks[..., 1]).reshape(seqs, dps, seqs, share)
    key_spot = key_spot.transpose(0, 2, 1, 3).reshape(seqs, rows)
    mine = lax.axis_index("seq")
    marks = kv_here[:, 2 * KVH * HD : 2 * KVH * HD + 2].astype(jnp.int32)
    q_spot = (marks[..., 0] * 32 + marks[..., 1]).reshape(dps, seqs, share)
    q_spot = q_spot.transpose(1, 0, 2).reshape(rows)
    unit = jnp.arange(units, dtype=jnp.int32)
    unit_first = UNIT * jnp.min(
        jnp.where(unit_ids[:, None] == unit_ids[None, :], unit[None, :], units), axis=1
    )

    def first_of(spots):
        hit = (spots // UNIT)[:, None] == unit[None, :]
        return jnp.sum(jnp.where(hit, unit_first[None, :], 0), axis=1)

    q_first = first_of(q_spot)
    flat = key_spot.reshape(group)
    cq, sq = turns(q_spot - q_first)
    ck, sk = turns(flat - first_of(flat))
    ck, sk = ck.reshape(seqs, rows, HD), sk.reshape(seqs, rows, HD)
    by_chunk = key_spot.reshape(seqs, seqs, chunk).transpose(1, 0, 2).reshape(group)
    kept = (by_chunk[None, :] <= q_spot[:, None]) & (by_chunk[None, :] >= q_first[:, None])
    bias = jnp.where(kept, 0.0, -1e30).astype(jnp.float32)

    whole2 = lambda *shape: pl.BlockSpec(shape, lambda h: (0,) * len(shape))
    out = pl.pallas_call(
        functools.partial(attend, seqs, dps),
        grid=(KVH,),
        in_specs=[
            pl.BlockSpec((rows, per_kv * HD), lambda h: (0, h)),
            pl.BlockSpec((seqs, rows, HD), lambda h: (0, 0, h)),
            pl.BlockSpec((seqs, rows, HD), lambda h: (0, 0, h + KVH)),
            whole2(rows, HD),
            whole2(rows, HD),
            whole2(seqs, rows, HD),
            whole2(seqs, rows, HD),
            whole2(rows, group),
        ],
        out_specs=pl.BlockSpec((rows, per_kv * HD), lambda h: (0, h)),
        out_shape=jax.ShapeDtypeStruct(queries.shape, jnp.bfloat16),
        scratch_shapes=[
            pltpu.VMEM((group, HD), jnp.bfloat16),
            pltpu.VMEM((group, HD), jnp.bfloat16),
            pltpu.VMEM((rows, per_kv * HD), jnp.bfloat16),
        ],
        compiler_params=pltpu.CompilerParams(vmem_limit_bytes=48 * 1024 * 1024),
    )(q_here, kv_all, kv_all, cq, sq, ck, sk, bias)
    home = swap(out)
    return lax.dot_general(
        onehot, home, (((0,), (0,)), ((), ())), preferred_element_type=jnp.float32
    ).astype(jnp.bfloat16)


def solution(mesh):
    return jax.shard_map(
        per_device,
        mesh=mesh,
        in_specs=(
            P(("dp", "seq"), None),
            P(("dp", "seq"), None),
            P(("dp", "seq"), None),
            P(("dp", "seq")),
            P(("dp", "seq")),
        ),
        out_specs=P(("dp", "seq"), None),
        check_vma=False,
    )
```

time: 504 us -> 214 us (0.42); the launches traced: 495 us -> 213 us
  blocking collectives: 248 us -> 82.5 us
  local copies, waits for them, and re-layouts: 84.7 us -> 1.7 us
  other arithmetic: 42.9 us -> 7.1 us
  Pallas kernels: 0 us -> 31.3 us
  matrix products: 30.4 us -> 10.5 us
  starting transfers between devices: 16.6 us -> 5.34 us
    all_gather x1 -> x0, blocking collectives: 100 us -> none  [per_device(): group_ids = lax.all_gather(segment_ids, 'seq', axis=0, tiled=True)]
    all_to_all x1 -> x2, blocking collectives: 148 us -> 72.6 us  [swap(): lax.all_to_all(x.reshape(dps, rows // dps, wide), 'dp', split_axis=0, con...]
    gather x8 -> x0, local copies, waits for them, and re-layouts: 43.8 us -> none  [the longest x1 12.2 us: per_device(): leaving = owner_out[where_rows].reshape(devices, share, -1)]
    all_gather x2 -> x1, waiting for transfers between devices: 23.6 us -> 60 us  [per_device(): kv_all = lax.all_gather(kv_here, 'seq', axis=0)]
    all_to_all x4 -> x1, waiting for transfers between devices: 34.7 us -> 0.01 us  [swap(): lax.all_to_all(x.reshape(dps, rows // dps, wide), 'dp', split_axis=0, con...]
    pallas_call x0 -> x1, Pallas kernels: none -> 31.3 us  [per_device(): pl.pallas_call(functools.partial(attend, seqs, dps), grid=(KVH,), in_spec...]
    dot_general x2 -> x3, matrix products: 30.4 us -> 10.5 us  [the longest x2 7.14 us: permuted(): jnp.dot(onehot, rows, preferred_element_type=jnp.float32)]
    reduce_sum x1 -> x3, other arithmetic: 15.7 us -> 0.34 us  [the longest x1 0.18 us: per_device(): slot = target * share + jnp.sum(same.astype(jnp.int32), axis=1)]
  transfers between devices with their start and end apart: 6 -> 2, of which waited for: 5 -> 1; matrix products, arithmetic and copies ran while one was open for 11% -> 6% of each run, Pallas kernels for 0% -> 0%
where the time goes in v1:
time: 214 us; the launch traced here: 213 us
  blocking collectives  82.5 us (39%)
  waiting for transfers between devices  60 us (28%)
  Pallas kernels  31.3 us (15%)
  between operations  14.2 us (7%)
  matrix products  10.5 us (5%)
  other arithmetic  7.1 us (3%)
  starting transfers between devices  5.34 us (2%)
    all_to_all x2, blocking collectives, swap(): lax.all_to_all(x.reshape(dps, rows // dps, wide), 'dp', split_axis=0, con...  72.6 us
    all_gather x1, waiting for transfers between devices, per_device(): kv_all = lax.all_gather(kv_here, 'seq', axis=0)  60 us
    pallas_call x1, Pallas kernels, per_device(): pl.pallas_call(functools.partial(attend, seqs, dps), grid=(KVH,), in_spec...  31.3 us
    unnamed x1, blocking collectives  9.91 us
    dot_general x2, matrix products, permuted(): jnp.dot(onehot, rows, preferred_element_type=jnp.float32)  7.14 us
    all_to_all x1, starting transfers between devices, swap(): lax.all_to_all(x.reshape(dps, rows // dps, wide), 'dp', split_axis=0, con...  5.34 us
  transfers between devices with their start and end apart: 2, of which 1 were waited for; matrix products, arithmetic and copies ran while one was open for 6% of the time, Pallas kernels for 0%

profile of v1, /device:TPU:1, one launch (start us, length us, event | category | flops | bytes accessed | tf_op | source)
XLA Modules:
  0.0 212.6 jit_solution(17920484387457447867)
XLA Ops:
  6.5 0.0 all-gather.2.cloned.1.call-start
  6.5 0.7 and_select_fusion.3
  7.2 0.2 convert_reduce_fusion
  7.4 0.1 select_convert_fusion
  7.6 1.7 convolution_convert_fusion.2
  9.3 20.4 %all_to_all.15 = bf16[8,32,2176]{2,1,0:T(8,128)(2,1)} all-to-all(bf16[8,32,2176]{2,1,0:T(8,128)(2,1)S(1)} %bitcast.24), channel_id=1, replica_groups=mesh['dp'=8,'seq'=4] {'dp'}, dimensions={0} | all-to-all | bytes 2228224 | tf_op jit(solution)/shard_map/all_to_all | solution.py:108
  29.7 0.0 all-gather.2.cloned.1.call-update
  29.7 5.5 %convolution_convert_fusion.1 = bf16[256,8192]{1,0:T(8,128)(2,1)} fusion(bf16[256,8192]{1,0:T(8,128)(2,1)} %param.5, s32[256]{0:T(256)S(1)} %get-tuple-element.15), kind=kOutput, calls=%fused_computation.1 | convolution fusion | flops 1075904512 | bytes 8389632 | tf_op jit(solution)/shard_map/dot_general | solution.py:24
  35.2 0.0 copy-start
  35.2 0.0 copy-start.1
  35.2 5.3 %all-to-all-start = ((bf16[8,32,8192]{2,1,0:T(8,128)(2,1)}), bf16[8,32,8192]{2,1,0:T(8,128)(2,1)}, u32[]{:S(2)}, u32[]{:S(2)}) async-start(bf16[8,32,8192]{2,1,0:T(8,128)(2,1)} %bitcast.20), calls=%async_computation | async-start | bytes 8388608 | tf_op jit(solution)/shard_map/all_to_all | solution.py:108
  40.5 0.0 copy-done
  40.5 0.1 slice.24
  40.6 0.0 copy-done.1
  40.6 0.7 dynamic-slice
  42.0 0.2 dynamic-update-slice
  42.2 9.9 %all-reduce = s32[8]{0:T(128)S(1)} all-reduce(s32[8]{0:T(128)S(1)} %dynamic-update-slice), channel_id=1, replica_groups=mesh['dp'=8,'seq'=4] {'seq'}, use_global_device_ids=true, to_apply=%add | all-reduce | flops 8 | bytes 64
  52.1 0.2 select_reduce_fusion.2
  52.3 0.9 slice_convert_fusion.1
  53.2 0.2 fusion.8
  53.4 0.1 add.43
  53.5 0.1 reshape.184
  53.6 0.1 select_reduce_fusion.1
  53.7 0.5 fusion.12
  54.2 0.1 pad_maximum_fusion.2.cq
  54.3 0.1 pad_maximum_fusion.3.sq
  54.4 60.0 %all-gather.2.cloned.1.call-done.k_ref.v_ref = bf16[4,256,2176]{2,1,0:T(8,128)(2,1)} async-done(((bf16[1,256,2176]{2,1,0:T(8,128)(2,1)}), bf16[4,256,2176]{2,1,0:T(8,128)(2,1)}) %all-gather.2.cloned.1.call-update) | async-done | bytes 4456464 | tf_op jit(solution)/shard_map/all_gather | solution.py:114
  114.4 1.0 slice_convert_fusion
  115.4 0.4 fusion.5
  115.8 0.1 add.45
  116.0 0.1 reshape_reshape.8
  116.1 0.1 reshape_reshape.9
  116.2 0.1 reshape_reshape.10
  116.3 0.1 select_reduce_fusion
  116.4 0.1 le.15
  116.5 1.9 fusion.7
  118.4 0.2 pad_maximum_fusion.ck
  118.6 0.2 pad_maximum_fusion.1.sk
  118.8 0.2 and_select_fusion.bias
  119.0 0.0 all-to-all-done
  119.0 31.3 %shard_map.55 = bf16[256,8192]{1,0:T(8,128)(2,1)} custom-call(bf16[256,8192]{1,0:T(8,128)(2,1)} %bitcast.1.q_ref, bf16[4,256,2176]{2,1,0:T(8,128)(2,1)} %all-gather.2.cloned.1.call-done.k_ref.v_ref, bf16[4,256,2176]{2,1,0:T(8,128)(2,1)} %all-gather.2.cloned.1.call-done.k_ref.v_ref, f32[256,128]{1,0:T(8,128)S(1)} %pad_maximum_fusion.2.cq, ...), custom_call_target="tpu_custom_call" | custom-call | tf_op jit(solution)/shard_map/pallas_call | solution.py:141
  150.3 52.2 %all_to_all.16 = bf16[8,32,8192]{2,1,0:T(8,128)(2,1)S(1)} all-to-all(bf16[8,32,8192]{2,1,0:T(8,128)(2,1)} %bitcast.19), channel_id=1, replica_groups=mesh['dp'=8,'seq'=4] {'dp'}, dimensions={0} | all-to-all | bytes 8388608 | tf_op jit(solution)/shard_map/all_to_all | solution.py:108
  202.4 3.3 %convolution_convert_fusion = bf16[256,8192]{1,0:T(8,128)(2,1)} fusion(bf16[256,8192]{1,0:T(8,128)(2,1)S(1)} %bitcast.21, s32[256]{0:T(256)S(1)} %get-tuple-element.15), kind=kOutput, calls=%fused_computation | convolution fusion | flops 1075904512 | bytes 8389632 | tf_op jit(solution)/shard_map/dot_general | solution.py:164
  (13 shorter events, 0.1 us)
Async XLA Ops:
  6.5 107.9 %all-gather.2.cloned.1.call-start = ((), (), s32[]{:S(2)}) async-start(), calls=%async_computation.3 | async-start | bytes 5570560 | tf_op jit(solution)/shard_map/all_gather | solution.py:114
  35.2 5.3 %copy-start = (s32[256]{0:T(256)S(1)}, s32[256]{0:T(256)}, u32[]{:S(2)}) copy-start(s32[256]{0:T(256)} %param.9) | copy-start | bytes 3076
  35.2 5.4 %copy-start.1 = (u32[32]{0:T(128)S(1)}, u32[32]{0:T(128)}, u32[]{:S(2)}) copy-start(u32[32]{0:T(128)} %constant.94) | copy-start | bytes 388
  35.2 83.8 %all-to-all-start = ((bf16[8,32,8192]{2,1,0:T(8,128)(2,1)}), bf16[8,32,8192]{2,1,0:T(8,128)(2,1)}, u32[]{:S(2)}, u32[]{:S(2)}) async-start(bf16[8,32,8192]{2,1,0:T(8,128)(2,1)} %bitcast.20), calls=%async_computation | async-start | bytes 8388608 | tf_op jit(solution)/shard_map/all_to_all | solution.py:108
Sparse Core Ops, SparseCore 0:
  29.8 84.5 all-gather.1

commit v2 on v1

v2 whole, which is shorter than its diff:
```python
import functools

import jax
import jax.numpy as jnp
from jax import lax
from jax.experimental import pallas as pl
from jax.experimental.pallas import tpu as pltpu
from jax.sharding import PartitionSpec as P

H = 64
KVH = 8
HD = 128
theta_base = 500000.0
UNIT = 128
META = 128
LOG2E = 1.4426950408889634


def onehot_rows(index, count):
    return (index[None, :] == jnp.arange(count, dtype=jnp.int32)[:, None]).astype(jnp.bfloat16)


def permuted(onehot, rows):
    return jnp.dot(onehot, rows, preferred_element_type=jnp.float32).astype(jnp.bfloat16)


def dot(a, b):
    return jnp.dot(a, b, preferred_element_type=jnp.float32)


def turn(x, c, s):
    return (x * c + pltpu.roll(x, HD // 2, 1) * s).astype(jnp.bfloat16)


def travel(
    seqs, dps, q, kv, seg, freqs, home,
    qr, kvz, metaz, ob, ks, vs, kmeta, cq, sq, ck, sk, bias, part_q,
    kv_send, kv_recv, kv_own, q_send, q_recv, q_own, o_send, o_recv, o_own,
    m_send, m_recv, m_own, mz_send, mz_recv, z_send, z_recv,
):
    rows = q.shape[0]
    per_kv = H // KVH
    wide = per_kv * HD
    chunk = rows // seqs
    share = chunk // dps
    slab = rows // dps
    group = rows * seqs
    upd = rows // UNIT
    me = lax.axis_index("dp")
    z = lax.axis_index("seq")

    def remote(src, dst, send, recv, where):
        return pltpu.make_async_remote_copy(
            src_ref=src, dst_ref=dst, send_sem=send, recv_sem=recv,
            device_id=where, device_id_type=pl.DeviceIdType.MESH,
        )

    barrier = pltpu.get_barrier_semaphore()
    peers = [lax.rem(me + k, dps) for k in range(1, dps)]
    planes = [lax.rem(z + k, seqs) for k in range(1, seqs)]
    for d in peers:
        pl.semaphore_signal(
            barrier, inc=1, device_id=(d, z), device_id_type=pl.DeviceIdType.MESH
        )
    for p in planes:
        pl.semaphore_signal(
            barrier, inc=1, device_id=(me, p), device_id_type=pl.DeviceIdType.MESH
        )
    pl.semaphore_wait(barrier, dps + seqs - 2)

    def slab_of(d):
        return pl.ds(pl.multiple_of(d * slab, slab), slab)

    def cols(h, width):
        return pl.ds(pl.multiple_of(h * width, width), width)

    meta_cols = pl.ds(2 * KVH * HD, META)
    most = pl.ds(0, rows - slab)
    for d in peers:
        remote(
            kv.at[slab_of(d), meta_cols], metaz.at[z, slab_of(me)], m_send, m_recv, (d, z)
        ).start()
    m_copy = pltpu.make_async_copy(
        kv.at[slab_of(me), meta_cols], metaz.at[z, slab_of(me)], m_own.at[0]
    )
    s_copy = pltpu.make_async_copy(seg, metaz.at[z, pl.ds(rows, 16)], m_own.at[1])
    m_copy.start()
    s_copy.start()

    def kv_local(h):
        return pltpu.make_async_copy(
            kv.at[slab_of(me), cols(h, 2 * HD)], kvz.at[z, h, slab_of(me)], kv_own.at[h]
        )

    def q_local(h):
        return pltpu.make_async_copy(
            q.at[slab_of(me), cols(h, wide)], qr.at[h, slab_of(me)], q_own.at[h]
        )

    def o_local(h):
        return pltpu.make_async_copy(
            ob.at[h, slab_of(me)], home.at[slab_of(me), cols(h, wide)], o_own.at[h]
        )

    @pl.loop(0, KVH)
    def _(h):
        for d in peers:
            remote(
                kv.at[slab_of(d), cols(h, 2 * HD)], kvz.at[z, h, slab_of(me)],
                kv_send.at[h], kv_recv.at[h], (d, z),
            ).start()
        kv_local(h).start()

    @pl.loop(0, KVH)
    def _(h):
        for d in peers:
            remote(
                q.at[slab_of(d), cols(h, wide)], qr.at[h, slab_of(me)],
                q_send.at[h], q_recv.at[h], (d, z),
            ).start()
        q_local(h).start()

    def meta_all():
        return remote(metaz.at[z, most], metaz.at[z, most], m_send, m_recv, (me, z))

    def kv_all(h):
        return remote(
            kvz.at[z, h, most], kvz.at[z, h, most], kv_send.at[h], kv_recv.at[h], (me, z)
        )

    def q_all(h):
        return remote(qr.at[h, most], qr.at[h, most], q_send.at[h], q_recv.at[h], (me, z))

    def o_all(h):
        place = home.at[most, cols(h, wide)]
        return remote(ob.at[h, most], place, o_send.at[h], o_recv.at[h], (me, z))

    meta_all().wait_recv()
    m_copy.wait()
    s_copy.wait()

    def meta_hop(k, p, origin):
        return remote(
            metaz.at[origin], metaz.at[origin], mz_send.at[k - 1], mz_recv.at[origin], (me, p)
        )

    for k, p in enumerate(planes, 1):
        meta_hop(k, p, z).start()

    def arrival(s):
        inner = s % chunk
        return (inner // share) * (seqs * share) + (s // chunk) * share + inner % share

    row = lax.broadcasted_iota(jnp.int32, (rows, rows), 0)
    col = lax.broadcasted_iota(jnp.int32, (rows, rows), 1)
    sort = jnp.where(col == arrival(row), 1.0, 0.0).astype(jnp.bfloat16)
    unsort = jnp.where(row == arrival(col), 1.0, 0.0).astype(jnp.bfloat16)

    def prepare():
        for k, p in enumerate(planes, 1):
            meta_hop(k, p, p).wait_recv()
        ids = []
        for p in range(seqs):
            line = metaz[p, rows : rows + 16, :].astype(jnp.float32)
            ids += [line[0:1, u : u + 1] for u in range(upd)]
        lane = lax.broadcasted_iota(jnp.int32, (1, META), 1)
        sign = jnp.where(lane < HD // 2, -1.0, 1.0)

        def spots(sorted_meta):
            spot = sorted_meta[:, 0:1] * 32.0 + sorted_meta[:, 1:2]
            mine = jnp.zeros_like(spot)
            for u in range(len(ids)):
                inside = (spot >= u * UNIT) & (spot < (u + 1) * UNIT)
                mine = jnp.where(inside, ids[u], mine)
            first = jnp.full_like(spot, float(group))
            for u in range(len(ids)):
                first = jnp.where(mine == ids[u], jnp.minimum(first, float(u * UNIT)), first)
            angles = (spot - first) * freqs[0:1, :]
            return spot, first, jnp.cos(angles), jnp.sin(angles) * sign

        for p in range(seqs):
            sorted_meta = dot(sort, metaz[p, :rows, :])
            _, _, ck[p], sk[p] = spots(sorted_meta)
            narrow = sorted_meta.astype(jnp.bfloat16)
            for c in range(seqs):
                kmeta[c * rows + p * chunk : c * rows + (p + 1) * chunk] = narrow[
                    c * chunk : (c + 1) * chunk
                ]
        spot, first, cq[...], sq[...] = spots(dot(sort, metaz[z, :rows, :]))
        weigh = jnp.where(lane == 0, 32.0, jnp.where(lane == 1, 1.0, 0.0))
        weigh = jnp.broadcast_to(weigh, (16, META)).astype(jnp.bfloat16)
        key = lax.dot_general(
            weigh, kmeta[...], (((1,), (1,)), ((), ())), preferred_element_type=jnp.float32
        )[0:1, :]
        bias[...] = jnp.where((key <= spot) & (key >= first), 0.0, -1e30)

    def attend(h):
        for p in range(seqs):
            both = dot(sort, kvz[p, h])
            part = turn(both[:, :HD], ck[p], sk[p])
            part_v = both[:, HD:].astype(jnp.bfloat16)
            for c in range(seqs):
                place = slice(c * rows + p * chunk, c * rows + (p + 1) * chunk)
                ks[place] = part[c * chunk : (c + 1) * chunk]
                vs[place] = part_v[c * chunk : (c + 1) * chunk]
        x = dot(sort, qr[h])
        turned = [turn(x[:, g * HD : (g + 1) * HD], cq[...], sq[...]) for g in range(per_kv)]
        for c in range(seqs):
            reach = (c + 1) * rows
            block = jnp.concatenate([t[c * chunk : (c + 1) * chunk] for t in turned], axis=0)
            s = lax.dot_general(
                block, ks[:reach], (((1,), (1,)), ((), ())), preferred_element_type=jnp.float32
            )
            s = s.reshape(per_kv, chunk, reach) * (HD ** -0.5 * LOG2E)
            s = s + bias[c * chunk : (c + 1) * chunk, :reach][None]
            e = jnp.exp2(s - jnp.max(s, axis=-1, keepdims=True))
            total = jnp.sum(e, axis=-1, keepdims=True).reshape(per_kv * chunk, 1)
            mixed = dot(e.astype(jnp.bfloat16).reshape(per_kv * chunk, reach), vs[:reach])
            mixed = (mixed / total).astype(jnp.bfloat16)
            for g in range(per_kv):
                part_q[c * chunk : (c + 1) * chunk, g * HD : (g + 1) * HD] = mixed[
                    g * chunk : (g + 1) * chunk
                ]
        ob[h] = dot(unsort, part_q[...]).astype(jnp.bfloat16)

    def hop(up, t, origin, h):
        step = 1 if up else -1
        return remote(
            kvz.at[origin, h], kvz.at[origin, h],
            z_send.at[(0 if up else 1) * seqs + t, h], z_recv.at[origin, h], (me, z + step),
        )

    @pl.loop(0, KVH + seqs - 1)
    def _(i):
        @pl.when(i < KVH)
        def _():
            kv_all(i).wait_recv()
            kv_local(i).wait()

            @pl.when(z + 1 < seqs)
            def _():
                hop(True, 0, z, i).start()

            @pl.when(z > 0)
            def _():
                hop(False, 0, z, i).start()

        for t in range(1, seqs):
            live = (i >= t) & (i - t < KVH)

            @pl.when(live & (z >= t))
            def _():
                hop(True, t, z - t, i - t).wait_recv()

                @pl.when(z + 1 < seqs)
                def _():
                    hop(True, t, z - t, i - t).start()

            @pl.when(live & (z + t < seqs))
            def _():
                hop(False, t, z + t, i - t).wait_recv()

                @pl.when(z > 0)
                def _():
                    hop(False, t, z + t, i - t).start()

        @pl.when(i == 1)
        def _():
            prepare()

        @pl.when(i >= seqs - 1)
        def _():
            h = i - (seqs - 1)
            q_all(h).wait_recv()
            q_local(h).wait()
            attend(h)
            for d in peers:
                remote(
                    ob.at[h, slab_of(d)], home.at[slab_of(me), cols(h, wide)],
                    o_send.at[h], o_recv.at[h], (d, z),
                ).start()
            o_local(h).start()

    meta_all().wait_send()
    for k, p in enumerate(planes, 1):
        meta_hop(k, p, z).wait_send()

    @pl.loop(0, KVH)
    def _(h):
        kv_all(h).wait_send()
        q_all(h).wait_send()
        for t in range(seqs - 1):

            @pl.when((z >= t) & (z + 1 < seqs))
            def _():
                hop(True, t, z - t, h).wait_send()

            @pl.when((z + t < seqs) & (z > 0))
            def _():
                hop(False, t, z + t, h).wait_send()

        o_all(h).wait_send()
        o_all(h).wait_recv()
        o_local(h).wait()


def per_device(queries, keys, values, plan, segment_ids):
    rows = queries.shape[0]
    seqs = lax.axis_size("seq")
    dps = lax.axis_size("dp")
    group = rows * seqs
    share = rows // (seqs * dps)
    chunk = rows // seqs
    per_kv = H // KVH
    target = plan // rows
    places = jnp.arange(rows, dtype=jnp.int32)
    same = (target[:, None] == target[None, :]) & (places[None, :] < places[:, None])
    slot = target * share + jnp.sum(same.astype(jnp.int32), axis=1)
    onehot = onehot_rows(slot, rows)
    spot = plan % group
    lane = jnp.arange(META, dtype=jnp.int32)[None, :]
    meta = jnp.where(lane == 0, (spot // 32)[:, None], jnp.where(lane == 1, (spot % 32)[:, None], 0))
    pairs = jnp.concatenate([keys.reshape(rows, KVH, HD), values.reshape(rows, KVH, HD)], axis=2)
    kv = jnp.concatenate([pairs.reshape(rows, 2 * KVH * HD), meta.astype(jnp.bfloat16)], axis=1)
    units = segment_ids[::UNIT]
    seg = jnp.zeros((16, META), jnp.bfloat16).at[0, : units.shape[0]].set(units.astype(jnp.bfloat16))
    exponents = jnp.arange(HD // 2, dtype=jnp.float32)
    freqs = theta_base ** (-2.0 * exponents / HD)
    freqs = jnp.broadcast_to(jnp.concatenate([freqs, freqs])[None, :], (8, HD))
    anywhere = pl.BlockSpec(memory_space=pl.ANY)
    inside = pl.BlockSpec(memory_space=pltpu.VMEM)
    dma = pltpu.SemaphoreType.DMA
    bf16, f32 = jnp.bfloat16, jnp.float32
    home = pl.pallas_call(
        functools.partial(travel, seqs, dps),
        in_specs=[anywhere, anywhere, inside, inside],
        out_specs=anywhere,
        out_shape=jax.ShapeDtypeStruct(queries.shape, bf16),
        scratch_shapes=[
            pltpu.VMEM((KVH, rows, per_kv * HD), bf16),
            pltpu.VMEM((seqs, KVH, rows, 2 * HD), bf16),
            pltpu.VMEM((seqs, rows + 16, META), bf16),
            pltpu.VMEM((KVH, rows, per_kv * HD), bf16),
            pltpu.VMEM((group, HD), bf16),
            pltpu.VMEM((group, HD), bf16),
            pltpu.VMEM((group, META), bf16),
            pltpu.VMEM((rows, HD), f32),
            pltpu.VMEM((rows, HD), f32),
            pltpu.VMEM((seqs, rows, HD), f32),
            pltpu.VMEM((seqs, rows, HD), f32),
            pltpu.VMEM((rows, group), f32),
            pltpu.VMEM((rows, per_kv * HD), bf16),
            dma((KVH,)), dma((KVH,)), dma((KVH,)),
            dma((KVH,)), dma((KVH,)), dma((KVH,)),
            dma((KVH,)), dma((KVH,)), dma((KVH,)),
            dma, dma, dma((2,)), dma((seqs,)), dma((seqs,)),
            dma((2 * seqs, KVH)), dma((seqs, KVH)),
        ],
        compiler_params=pltpu.CompilerParams(
            collective_id=0, has_side_effects=True, vmem_limit_bytes=56 * 1024 * 1024
        ),
    )(permuted(onehot, queries), permuted(onehot, kv), seg, freqs)
    return lax.dot_general(
        onehot, home, (((0,), (0,)), ((), ())), preferred_element_type=jnp.float32
    ).astype(jnp.bfloat16)


def solution(mesh):
    return jax.shard_map(
        per_device,
        mesh=mesh,
        in_specs=(
            P(("dp", "seq"), None),
            P(("dp", "seq"), None),
            P(("dp", "seq"), None),
            P(("dp", "seq")),
            P(("dp", "seq")),
        ),
        out_specs=P(("dp", "seq"), None),
        check_vma=False,
    )
```

time: 214 us -> 127 us (0.59)
  blocking collectives: 82.5 us -> 0 us
  Pallas kernels: 31.3 us -> 111 us
  waiting for transfers between devices: 60 us -> 0 us
  between operations: 14.2 us -> 0.06 us
  starting transfers between devices: 5.34 us -> 0 us
  other arithmetic: 7.1 us -> 1.91 us
  local copies, waits for them, and re-layouts: 1.7 us -> 4.12 us
    pallas_call x1, Pallas kernels: 31.3 us -> 111 us  [per_device(): pl.pallas_call(functools.partial(travel, seqs, dps), in_specs=[anywhere,...]
    all_to_all x2 -> x0, blocking collectives: 72.6 us -> none  [swap(): lax.all_to_all(x.reshape(dps, rows // dps, wide), 'dp', split_axis=0, con...]
    all_gather x1 -> x0, waiting for transfers between devices: 60 us -> none  [per_device(): kv_all = lax.all_gather(kv_here, 'seq', axis=0)]
    unnamed x1 -> x0, blocking collectives: 9.91 us -> none
    all_to_all x1 -> x0, starting transfers between devices: 5.34 us -> none  [swap(): lax.all_to_all(x.reshape(dps, rows // dps, wide), 'dp', split_axis=0, con...]
    neg x2 -> x0, other arithmetic: 2.44 us -> none  [turns(): -sine]
    dot_general x2, matrix products: 7.14 us -> 4.76 us  [permuted(): jnp.dot(onehot, rows, preferred_element_type=jnp.float32)]
    dot_general x1, matrix products: 3.32 us -> 5.51 us  [per_device(): lax.dot_general(onehot, home, (((0,), (0,)), ((), ())), preferred_element...]
  transfers between devices with their start and end apart: 2 -> 0, of which waited for: 1 -> 0; matrix products, arithmetic and copies ran while one was open for 6% -> 0% of each run, Pallas kernels for 0% -> 0%
where the time goes in v2:
time: 127 us
  Pallas kernels  111 us (87%)
  matrix products  10.3 us (8%)
  local copies, waits for them, and re-layouts  4.12 us (3%)
  other arithmetic  1.91 us (2%)
    pallas_call x1, Pallas kernels, per_device(): pl.pallas_call(functools.partial(travel, seqs, dps), in_specs=[anywhere,...  111 us
    dot_general x1, matrix products, per_device(): lax.dot_general(onehot, home, (((0,), (0,)), ((), ())), preferred_element...  5.51 us
    dot_general x2, matrix products, permuted(): jnp.dot(onehot, rows, preferred_element_type=jnp.float32)  4.76 us
    unnamed x5, local copies, waits for them, and re-layouts  2.84 us

profile of v2, /device:TPU:1, one launch (start us, length us, event | category | flops | bytes accessed | tf_op | source)
XLA Modules:
  0.0 127.1 jit_solution(8297240677709675281)
XLA Ops:
  0.0 0.7 convert.3
  0.7 0.1 slice.20
  0.8 0.1 pad_maximum_fusion.1
  0.9 0.7 and_select_fusion.1
  1.6 0.2 convert_reduce_fusion
  1.8 0.6 broadcast_in_dim.57.freqs
  2.4 0.6 scatter.4.seg
  3.0 0.1 select_convert_fusion
  3.1 0.0 copy-start
  3.1 1.3 %copy.6 = bf16[32,8,8,128]{3,2,1,0:T(8,128)(2,1)S(1)} copy(bf16[32,8,8,128]{3,1,2,0:T(8,128)(2,1)} %bitcast.13) | data formatting | bytes 1048576
  4.4 1.2 copy.7
  5.7 0.1 pad_maximum_fusion
  5.8 0.3 copy.8
  6.1 1.5 %convolution_convert_fusion.2.kv = bf16[256,2176]{1,0:T(8,128)(2,1)} fusion(bf16[256,128]{1,0:T(8,128)(2,1)S(1)} %select_convert_fusion, bf16[256,2048]{1,0:T(8,128)(2,1)S(1)} %bitcast.12, s32[256]{0:T(256)S(1)} %get-tuple-element.21), kind=kOutput, calls=%fused_computation.2 | convolution fusion | flops 288063488 | bytes 2229248 | tf_op jit(solution)/shard_map/dot_general | solution.py:24
  7.6 0.0 copy-done
  7.6 3.3 %convolution_convert_fusion.1.q = bf16[256,8192]{1,0:T(8,128)(2,1)} fusion(bf16[256,8192]{1,0:T(8,128)(2,1)S(1)} %copy-done, s32[256]{0:T(256)S(1)} %get-tuple-element.21), kind=kOutput, calls=%fused_computation.1 | convolution fusion | flops 1075904512 | bytes 8389632 | tf_op jit(solution)/shard_map/dot_general | solution.py:24
  10.8 110.8 %shard_map.55 = bf16[256,8192]{1,0:T(8,128)(2,1)} custom-call(bf16[256,8192]{1,0:T(8,128)(2,1)} %convolution_convert_fusion.1.q, bf16[256,2176]{1,0:T(8,128)(2,1)} %convolution_convert_fusion.2.kv, bf16[16,128]{1,0:T(8,128)(2,1)} %scatter.4.seg, f32[8,128]{1,0:T(8,128)} %broadcast_in_dim.57.freqs), custom_call_target="tpu_custom_call" | custom-call | tf_op jit(solution)/shard_map/pallas_call | solution.py:334
  121.6 5.5 %convolution_convert_fusion = bf16[256,8192]{1,0:T(8,128)(2,1)} fusion(bf16[256,8192]{1,0:T(8,128)(2,1)} %shard_map.55, s32[256]{0:T(256)S(1)} %get-tuple-element.21), kind=kOutput, calls=%fused_computation | convolution fusion | flops 1075904512 | bytes 8389632 | tf_op jit(solution)/shard_map/dot_general | solution.py:363
  (3 shorter events, 0.0 us)
Async XLA Ops:
  3.1 4.5 %copy-start = (bf16[256,8192]{1,0:T(8,128)(2,1)S(1)}, bf16[256,8192]{1,0:T(8,128)(2,1)}, u32[]{:S(2)}) copy-start(bf16[256,8192]{1,0:T(8,128)(2,1)} %param.7) | copy-start | bytes 12582916

commit v3 on v2

--- a/solution.py
+++ b/solution.py
@@ -2,6 +2,7 @@
 
 import jax
 import jax.numpy as jnp
+import numpy as np
 from jax import lax
 from jax.experimental import pallas as pl
 from jax.experimental.pallas import tpu as pltpu
@@ -16,14 +17,6 @@
 LOG2E = 1.4426950408889634
 
 
-def onehot_rows(index, count):
-    return (index[None, :] == jnp.arange(count, dtype=jnp.int32)[:, None]).astype(jnp.bfloat16)
-
-
-def permuted(onehot, rows):
-    return jnp.dot(onehot, rows, preferred_element_type=jnp.float32).astype(jnp.bfloat16)
-
-
 def dot(a, b):
     return jnp.dot(a, b, preferred_element_type=jnp.float32)
 
@@ -32,10 +25,16 @@
     return (x * c + pltpu.roll(x, HD // 2, 1) * s).astype(jnp.bfloat16)
 
 
+def restore(onehot, home, out):
+    out[...] = lax.dot_general(
+        onehot[...], home[...], (((0,), (0,)), ((), ())), preferred_element_type=jnp.float32
+    ).astype(jnp.bfloat16)
+
+
 def travel(
-    seqs, dps, q, kv, seg, freqs, home,
-    qr, kvz, metaz, ob, ks, vs, kmeta, cq, sq, ck, sk, bias, part_q,
-    kv_send, kv_recv, kv_own, q_send, q_recv, q_own, o_send, o_recv, o_own,
+    seqs, dps, q, k, v, plan, seg, freqs, home, onehot,
+    qs, kvs, metas, qr, kvz, metaz, ob, ks, vs, kmeta, cq, sq, ck, sk, bias, part_q,
+    kv_send, kv_recv, kv_own, q_send, q_recv, q_own, q_load, o_send, o_recv, o_own,
     m_send, m_recv, m_own, mz_send, mz_recv, z_send, z_recv,
 ):
     rows = q.shape[0]
@@ -55,6 +54,12 @@
             device_id=where, device_id_type=pl.DeviceIdType.MESH,
         )
 
+    def slab_of(d):
+        return pl.ds(pl.multiple_of(d * slab, slab), slab)
+
+    def cols(h, width):
+        return pl.ds(pl.multiple_of(h * width, width), width)
+
     barrier = pltpu.get_barrier_semaphore()
     peers = [lax.rem(me + k, dps) for k in range(1, dps)]
     planes = [lax.rem(z + k, seqs) for k in range(1, seqs)]
@@ -66,35 +71,56 @@
         pl.semaphore_signal(
             barrier, inc=1, device_id=(me, p), device_id_type=pl.DeviceIdType.MESH
         )
+
+    def q_in(h):
+        return pltpu.make_async_copy(q.at[:, cols(h, wide)], qs.at[h], q_load.at[h])
+
+    @pl.loop(0, KVH)
+    def _(h):
+        q_in(h).start()
+
+    row = lax.broadcasted_iota(jnp.int32, (rows, rows), 0)
+    col = lax.broadcasted_iota(jnp.int32, (rows, rows), 1)
+    eye = jnp.where(row == col, 1.0, 0.0).astype(jnp.bfloat16)
+    target = (plan[...] // rows).astype(jnp.float32)
+    spread = jnp.broadcast_to(target, (16, rows)).astype(jnp.bfloat16)
+    across = (((1,), (1,)), ((), ()))
+    upright = lax.dot_general(eye, spread, across, preferred_element_type=jnp.float32)[:, 0:1]
+    ahead = jnp.where((upright == target) & (row < col), 1.0, 0.0)
+    slot = target * share + jnp.sum(ahead, axis=0, keepdims=True)
+    onehot[...] = jnp.where(slot == row.astype(jnp.float32), 1.0, 0.0).astype(jnp.bfloat16)
+    spot_row = plan[...] % group
+    lines = lax.broadcasted_iota(jnp.int32, (META, rows), 0)
+    high = (spot_row // 32).astype(jnp.float32)
+    low = (spot_row % 32).astype(jnp.float32)
+    lines = jnp.where(lines == 0, high, jnp.where(lines == 1, low, 0.0)).astype(jnp.bfloat16)
+    metas[...] = lax.dot_general(
+        onehot[...], lines, across, preferred_element_type=jnp.float32
+    ).astype(jnp.bfloat16)
+    lane = lax.broadcasted_iota(jnp.int32, (1, META), 1)
+    marks = jnp.zeros((1, META), jnp.float32)
+    for u in range(upd):
+        marks = jnp.where(lane == u, seg[0:1, u * UNIT : u * UNIT + 1].astype(jnp.float32), marks)
+    metaz[z, rows : rows + 16, :] = jnp.broadcast_to(marks, (16, META)).astype(jnp.bfloat16)
+
     pl.semaphore_wait(barrier, dps + seqs - 2)
 
-    def slab_of(d):
-        return pl.ds(pl.multiple_of(d * slab, slab), slab)
-
-    def cols(h, width):
-        return pl.ds(pl.multiple_of(h * width, width), width)
-
-    meta_cols = pl.ds(2 * KVH * HD, META)
     most = pl.ds(0, rows - slab)
     for d in peers:
         remote(
-            kv.at[slab_of(d), meta_cols], metaz.at[z, slab_of(me)], m_send, m_recv, (d, z)
+            metas.at[slab_of(d)], metaz.at[z, slab_of(me)], m_send, m_recv, (d, z)
         ).start()
-    m_copy = pltpu.make_async_copy(
-        kv.at[slab_of(me), meta_cols], metaz.at[z, slab_of(me)], m_own.at[0]
-    )
-    s_copy = pltpu.make_async_copy(seg, metaz.at[z, pl.ds(rows, 16)], m_own.at[1])
+    m_copy = pltpu.make_async_copy(metas.at[slab_of(me)], metaz.at[z, slab_of(me)], m_own)
     m_copy.start()
-    s_copy.start()
 
     def kv_local(h):
         return pltpu.make_async_copy(
-            kv.at[slab_of(me), cols(h, 2 * HD)], kvz.at[z, h, slab_of(me)], kv_own.at[h]
+            kvs.at[h, slab_of(me)], kvz.at[z, h, slab_of(me)], kv_own.at[h]
         )
 
     def q_local(h):
         return pltpu.make_async_copy(
-            q.at[slab_of(me), cols(h, wide)], qr.at[h, slab_of(me)], q_own.at[h]
+            qs.at[h, slab_of(me)], qr.at[h, slab_of(me)], q_own.at[h]
         )
 
     def o_local(h):
@@ -104,18 +130,21 @@
 
     @pl.loop(0, KVH)
     def _(h):
+        both = jnp.concatenate([k[:, cols(h, HD)], v[:, cols(h, HD)]], axis=1)
+        kvs[h] = dot(onehot[...], both).astype(jnp.bfloat16)
         for d in peers:
             remote(
-                kv.at[slab_of(d), cols(h, 2 * HD)], kvz.at[z, h, slab_of(me)],
+                kvs.at[h, slab_of(d)], kvz.at[z, h, slab_of(me)],
                 kv_send.at[h], kv_recv.at[h], (d, z),
             ).start()
         kv_local(h).start()
 
-    @pl.loop(0, KVH)
-    def _(h):
+    def q_out(h):
+        q_in(h).wait()
+        qs[h] = dot(onehot[...], qs[h]).astype(jnp.bfloat16)
         for d in peers:
             remote(
-                q.at[slab_of(d), cols(h, wide)], qr.at[h, slab_of(me)],
+                qs.at[h, slab_of(d)], qr.at[h, slab_of(me)],
                 q_send.at[h], q_recv.at[h], (d, z),
             ).start()
         q_local(h).start()
@@ -137,7 +166,6 @@
 
     meta_all().wait_recv()
     m_copy.wait()
-    s_copy.wait()
 
     def meta_hop(k, p, origin):
         return remote(
@@ -151,8 +179,6 @@
         inner = s % chunk
         return (inner // share) * (seqs * share) + (s // chunk) * share + inner % share
 
-    row = lax.broadcasted_iota(jnp.int32, (rows, rows), 0)
-    col = lax.broadcasted_iota(jnp.int32, (rows, rows), 1)
     sort = jnp.where(col == arrival(row), 1.0, 0.0).astype(jnp.bfloat16)
     unsort = jnp.where(row == arrival(col), 1.0, 0.0).astype(jnp.bfloat16)
 
@@ -163,7 +189,6 @@
         for p in range(seqs):
             line = metaz[p, rows : rows + 16, :].astype(jnp.float32)
             ids += [line[0:1, u : u + 1] for u in range(upd)]
-        lane = lax.broadcasted_iota(jnp.int32, (1, META), 1)
         sign = jnp.where(lane < HD // 2, -1.0, 1.0)
 
         def spots(sorted_meta):
@@ -264,7 +289,12 @@
                 def _():
                     hop(False, t, z + t, i - t).start()
 
-        @pl.when(i == 1)
+        @pl.when(i < KVH // 2)
+        def _():
+            q_out(2 * i)
+            q_out(2 * i + 1)
+
+        @pl.when(i == min(2, seqs - 1))
         def _():
             prepare()
 
@@ -312,31 +342,25 @@
     share = rows // (seqs * dps)
     chunk = rows // seqs
     per_kv = H // KVH
-    target = plan // rows
-    places = jnp.arange(rows, dtype=jnp.int32)
-    same = (target[:, None] == target[None, :]) & (places[None, :] < places[:, None])
-    slot = target * share + jnp.sum(same.astype(jnp.int32), axis=1)
-    onehot = onehot_rows(slot, rows)
-    spot = plan % group
-    lane = jnp.arange(META, dtype=jnp.int32)[None, :]
-    meta = jnp.where(lane == 0, (spot // 32)[:, None], jnp.where(lane == 1, (spot % 32)[:, None], 0))
-    pairs = jnp.concatenate([keys.reshape(rows, KVH, HD), values.reshape(rows, KVH, HD)], axis=2)
-    kv = jnp.concatenate([pairs.reshape(rows, 2 * KVH * HD), meta.astype(jnp.bfloat16)], axis=1)
-    units = segment_ids[::UNIT]
-    seg = jnp.zeros((16, META), jnp.bfloat16).at[0, : units.shape[0]].set(units.astype(jnp.bfloat16))
-    exponents = jnp.arange(HD // 2, dtype=jnp.float32)
-    freqs = theta_base ** (-2.0 * exponents / HD)
-    freqs = jnp.broadcast_to(jnp.concatenate([freqs, freqs])[None, :], (8, HD))
+    exponents = np.arange(HD // 2, dtype=np.float32)
+    freqs = np.float32(theta_base) ** (np.float32(-2.0) * exponents / np.float32(HD))
+    freqs = jnp.asarray(np.broadcast_to(np.concatenate([freqs, freqs])[None, :], (8, HD)))
     anywhere = pl.BlockSpec(memory_space=pl.ANY)
     inside = pl.BlockSpec(memory_space=pltpu.VMEM)
     dma = pltpu.SemaphoreType.DMA
     bf16, f32 = jnp.bfloat16, jnp.float32
-    home = pl.pallas_call(
+    home, onehot = pl.pallas_call(
         functools.partial(travel, seqs, dps),
-        in_specs=[anywhere, anywhere, inside, inside],
-        out_specs=anywhere,
-        out_shape=jax.ShapeDtypeStruct(queries.shape, bf16),
+        in_specs=[anywhere, inside, inside, inside, inside, inside],
+        out_specs=(anywhere, inside),
+        out_shape=(
+            jax.ShapeDtypeStruct(queries.shape, bf16),
+            jax.ShapeDtypeStruct((rows, rows), bf16),
+        ),
         scratch_shapes=[
+            pltpu.VMEM((KVH, rows, per_kv * HD), bf16),
+            pltpu.VMEM((KVH, rows, 2 * HD), bf16),
+            pltpu.VMEM((rows, META), bf16),
             pltpu.VMEM((KVH, rows, per_kv * HD), bf16),
             pltpu.VMEM((seqs, KVH, rows, 2 * HD), bf16),
             pltpu.VMEM((seqs, rows + 16, META), bf16),
@@ -352,17 +376,22 @@
             pltpu.VMEM((rows, per_kv * HD), bf16),
             dma((KVH,)), dma((KVH,)), dma((KVH,)),
             dma((KVH,)), dma((KVH,)), dma((KVH,)),
-            dma((KVH,)), dma((KVH,)), dma((KVH,)),
-            dma, dma, dma((2,)), dma((seqs,)), dma((seqs,)),
+            dma((KVH,)), dma((KVH,)), dma((KVH,)), dma((KVH,)),
+            dma, dma, dma, dma((seqs,)), dma((seqs,)),
             dma((2 * seqs, KVH)), dma((seqs, KVH)),
         ],
         compiler_params=pltpu.CompilerParams(
             collective_id=0, has_side_effects=True, vmem_limit_bytes=56 * 1024 * 1024
         ),
-    )(permuted(onehot, queries), permuted(onehot, kv), seg, freqs)
-    return lax.dot_general(
-        onehot, home, (((0,), (0,)), ((), ())), preferred_element_type=jnp.float32
-    ).astype(jnp.bfloat16)
+    )(queries, keys, values, plan[None, :], segment_ids[None, :], freqs)
+    block = pl.BlockSpec((rows, per_kv * HD), lambda h: (0, h))
+    return pl.pallas_call(
+        restore,
+        grid=(KVH,),
+        in_specs=[pl.BlockSpec((rows, rows), lambda h: (0, 0)), block],
+        out_specs=block,
+        out_shape=jax.ShapeDtypeStruct(queries.shape, bf16),
+    )(onehot, home)
 
 
 def solution(mesh):

time: 127 us -> 121 us (0.953)
  matrix products: 10.3 us -> 0 us
  Pallas kernels: 111 us -> 119 us
  local copies, waits for them, and re-layouts: 4.12 us -> 1.25 us
  other arithmetic: 1.91 us -> 0 us
    dot_general x3 -> x0, matrix products: 10.3 us -> none  [the longest x1 5.51 us: per_device(): lax.dot_general(onehot, home, (((0,), (0,)), ((), ())), preferred_element...]
    pallas_call x0 -> x1, Pallas kernels: none -> 7.58 us  [per_device(): pl.pallas_call(restore, grid=(KVH,), in_specs=[pl.BlockSpec((rows, rows),...]
    unnamed x5 -> x0, local copies, waits for them, and re-layouts: 2.84 us -> none
where the time goes in v3:
time: 121 us
  Pallas kernels  119 us (98%)
  local copies, waits for them, and re-layouts  1.25 us (1%)
    pallas_call x1, Pallas kernels, per_device(): pl.pallas_call(functools.partial(travel, seqs, dps), in_specs=[anywhere,...  112 us
    pallas_call x1, Pallas kernels, per_device(): pl.pallas_call(restore, grid=(KVH,), in_specs=[pl.BlockSpec((rows, rows),...  7.58 us

profile of v3, /device:TPU:1, one launch (start us, length us, event | category | flops | bytes accessed | tf_op | source)
XLA Modules:
  0.0 120.7 jit_solution(2794263874513963063)
XLA Ops:
  0.0 1.2 %jit_solution_.3.freqs = f32[8,128]{1,0:T(8,128)} broadcast(f32[128]{0:T(128)} %constant.2.clone), dimensions={1} | broadcast | bytes 4608 | tf_op jit(solution)
  1.2 111.8 %shard_map.64 = (bf16[256,8192]{1,0:T(8,128)(2,1)}, bf16[256,256]{1,0:T(8,128)(2,1)}) custom-call(bf16[256,8192]{1,0:T(8,128)(2,1)} %q.1, bf16[256,1024]{1,0:T(8,128)(2,1)} %k.1, bf16[256,1024]{1,0:T(8,128)(2,1)} %v.1, s32[1,256]{1,0:T(1,128)} %bitcast.2, s32[1,256]{1,0:T(1,128)} %bitcast.3, f32[8,128]{1,0:T(8,128)} %jit_solution_.3.freqs), custom_call_target="tpu_custom_call" | custom-call | tf_op jit(solution)/shard_map/pallas_call | solution.py:352
  113.1 7.6 %shard_map.65 = bf16[256,8192]{1,0:T(8,128)(2,1)} custom-call(bf16[256,256]{1,0:T(8,128)(2,1)} %get-tuple-element.7.onehot, bf16[256,8192]{1,0:T(8,128)(2,1)} %get-tuple-element.8.home), custom_call_target="tpu_custom_call" | custom-call | tf_op jit(solution)/shard_map/pallas_call | solution.py:388

commit v4 on v3

--- a/solution.py
+++ b/solution.py
@@ -13,6 +13,7 @@
 HD = 128
 theta_base = 500000.0
 UNIT = 128
+AHEAD = 2
 META = 128
 LOG2E = 1.4426950408889634
 
@@ -257,18 +258,20 @@
 
     @pl.loop(0, KVH + seqs - 1)
     def _(i):
-        @pl.when(i < KVH)
+        @pl.when(i < KVH // AHEAD)
         def _():
-            kv_all(i).wait_recv()
-            kv_local(i).wait()
-
-            @pl.when(z + 1 < seqs)
-            def _():
-                hop(True, 0, z, i).start()
-
-            @pl.when(z > 0)
-            def _():
-                hop(False, 0, z, i).start()
+            for n in range(AHEAD):
+                h = i * AHEAD + n
+                kv_all(h).wait_recv()
+                kv_local(h).wait()
+
+                @pl.when(z + 1 < seqs)
+                def _():
+                    hop(True, 0, z, h).start()
+
+                @pl.when(z > 0)
+                def _():
+                    hop(False, 0, z, h).start()
 
         for t in range(1, seqs):
             live = (i >= t) & (i - t < KVH)

time: 121 us -> 121 us (level)
  no operation moved by 1% of the time
where the time goes in v4:
time: 121 us
  Pallas kernels  119 us (98%)
  local copies, waits for them, and re-layouts  1.25 us (1%)
    pallas_call x1, Pallas kernels, per_device(): pl.pallas_call(functools.partial(travel, seqs, dps), in_specs=[anywhere,...  112 us
    pallas_call x1, Pallas kernels, per_device(): pl.pallas_call(restore, grid=(KVH,), in_specs=[pl.BlockSpec((rows, rows),...  7.58 us

profile of v4, /device:TPU:1, one launch (start us, length us, event | category | flops | bytes accessed | tf_op | source)
XLA Modules:
  0.0 120.7 jit_solution(8591835743288451000)
XLA Ops:
  0.0 1.2 %jit_solution_.3.freqs = f32[8,128]{1,0:T(8,128)} broadcast(f32[128]{0:T(128)} %constant.2.clone), dimensions={1} | broadcast | bytes 4608 | tf_op jit(solution)
  1.2 111.8 %shard_map.64 = (bf16[256,8192]{1,0:T(8,128)(2,1)}, bf16[256,256]{1,0:T(8,128)(2,1)}) custom-call(bf16[256,8192]{1,0:T(8,128)(2,1)} %q.1, bf16[256,1024]{1,0:T(8,128)(2,1)} %k.1, bf16[256,1024]{1,0:T(8,128)(2,1)} %v.1, s32[1,256]{1,0:T(1,128)} %bitcast.2, s32[1,256]{1,0:T(1,128)} %bitcast.3, f32[8,128]{1,0:T(8,128)} %jit_solution_.3.freqs), custom_call_target="tpu_custom_call" | custom-call | tf_op jit(solution)/shard_map/pallas_call | solution.py:355
  113.1 7.6 %shard_map.65 = bf16[256,8192]{1,0:T(8,128)(2,1)} custom-call(bf16[256,256]{1,0:T(8,128)(2,1)} %get-tuple-element.7.onehot, bf16[256,8192]{1,0:T(8,128)(2,1)} %get-tuple-element.8.home), custom_call_target="tpu_custom_call" | custom-call | tf_op jit(solution)/shard_map/pallas_call | solution.py:391
